TPU v7x, 32 devices: a whole 2x2x4 slice. The times are simulated.
32 devices in a mesh: img: 8 (over y, x, core), feat: 4 (over z).
Axes of the slice: x: 2, y: 2, z: 4, core: 2. Of those that a mesh axis runs over, the one named last changes fastest.
Arguments:
- coeffs: bfloat16 [16384, 512], P('img', 'feat'), may hold values from -16 to 16
- triples: int32 [3, 16384], P(None, 'feat'), may hold values from 0 to 510, as said below
- sketch: int32 [16384, 128], P('feat'), may hold values from -1 to 1
Outputs:
- basis: float32 [16384, 128], P('img')
- projected: float32 [128, 16384], P('img', 'feat')
Inputs may be any that keep to these rules, and one draw needn't show every extreme that they name: `triples`: every column is a triple k1, k2, k1 + k2 with k1 and k2 below 256.
All inputs are finite; a program needn't handle non-finite values.
Results may differ from a plain program's by a relative error of at most 0.0044.
Values may be sent and summed in bfloat16 or wider, within the bound.
A program may use at most 192 MiB of HBM per device.

v0:
```python
import functools

import jax
import jax.numpy as jnp
from jax import lax
from jax.experimental import pallas as pl
from jax.experimental.pallas import tpu as pltpu
from jax.sharding import PartitionSpec as P

CHUNKS = 8
MESH = pl.DeviceIdType.MESH
VMEM = pl.BlockSpec(memory_space=pltpu.VMEM)


def greet(axis, peers):
    barrier = pltpu.get_barrier_semaphore()
    for peer in peers:
        pl.semaphore_signal(barrier, inc=1, device_id={axis: peer}, device_id_type=MESH)
    pl.semaphore_wait(barrier, len(peers))


def gather_kernel(
    count, width, coeffs_ref, triples_ref, sketch_ref, tile_ref, value_ref, blocks, sel_ref, signs_ref,
    sum_ref, part_ref, slots, full_ref, own_sem, send_sem, recv_sem, to_sem, from_sem, out_sem, in_sem
):
    me = lax.axis_index("feat")
    rows, part = coeffs_ref.shape
    step = rows // CHUNKS
    half = count * part // 2
    tiles = sketch_ref.shape[0] // width
    spans = ((0, half), (half, half), (2 * half, 2 * half))

    def build(index):
        start, depth = spans[index]

        def one(j, carry):
            cols = pl.ds(pl.multiple_of(j * width, width), width)
            levels = lax.broadcasted_iota(jnp.int32, (depth, width), 0)
            chosen = triples_ref[index : index + 1, cols]
            sel_ref[start : start + depth, cols] = jnp.where(levels == chosen, 1.0, 0.0).astype(jnp.bfloat16)
            if index == 0:
                signs_ref[cols, :] = sketch_ref[cols, :].astype(jnp.float32).astype(jnp.bfloat16)
            return carry

        lax.fori_loop(0, tiles, one, 0)

    own = pltpu.make_async_copy(coeffs_ref, blocks.at[me], own_sem)
    own.start()
    peers = peers_of(me, count)
    piece = step // count
    greet("feat", peers)
    own.wait()

    def copy(side, hop, chunk, source, target):
        span = blocks.at[source, pl.ds(pl.multiple_of(chunk * step, step), step)]
        return pltpu.make_async_remote_copy(
            src_ref=span,
            dst_ref=span,
            send_sem=send_sem.at[side, hop, chunk],
            recv_sem=recv_sem.at[side, hop, chunk],
            device_id={"feat": target},
            device_id_type=MESH,
        )

    def rows_of(chunk, owner):
        return pl.ds(pl.multiple_of(chunk * step + owner * piece, piece), piece)

    def reduce_copy(k, chunk):
        return pltpu.make_async_remote_copy(
            src_ref=part_ref.at[rows_of(chunk, peers[k])],
            dst_ref=slots.at[k, chunk],
            send_sem=to_sem.at[k, chunk],
            recv_sem=from_sem.at[k, chunk],
            device_id={"feat": peers[k]},
            device_id_type=MESH,
        )

    def spread_copy(k, chunk, owner):
        span = full_ref.at[rows_of(chunk, owner)]
        return pltpu.make_async_remote_copy(
            src_ref=span,
            dst_ref=span,
            send_sem=out_sem.at[k, chunk],
            recv_sem=in_sem.at[k, chunk],
            device_id={"feat": peers[k]},
            device_id_type=MESH,
        )

    def one_round(turn, carry):
        for hop in range(count):
            chunk = turn - hop
            live = (chunk >= 0) & (chunk < CHUNKS)
            if hop > 0:

                @pl.when(live & (me >= hop))
                def _():
                    copy(0, hop - 1, chunk, me - hop, me - 1).wait_recv()

                @pl.when(live & (me + hop < count))
                def _():
                    copy(1, hop - 1, chunk, me + hop, me + 1).wait_recv()

            if hop < count - 1:

                @pl.when(live & (me >= hop) & (me < count - 1))
                def _():
                    copy(0, hop, chunk, me - hop, me + 1).start()

                @pl.when(live & (me + hop < count) & (me > 0))
                def _():
                    copy(1, hop, chunk, me + hop, me - 1).start()

        for index in range(3):

            @pl.when(turn == min(index, count - 2))
            def _():
                build(index)

        base = turn - (count - 1)

        @pl.when((base >= 1) & (base <= CHUNKS))
        def _():
            for k in range(count - 1):
                reduce_copy(k, base - 1).start()

        @pl.when(base >= 2)
        def _():
            for k in range(count - 1):
                spread_copy(k, base - 2, me).start()

        @pl.when((base >= 0) & (base < CHUNKS))
        def _():
            first_row = pl.multiple_of(base * step, step)
            here = pl.ds(first_row, step)
            sum_ref[...] = jnp.zeros(sum_ref.shape, jnp.float32)
            low = jnp.concatenate([blocks[s, here, :] for s in range(count // 2)], axis=1)
            high = jnp.concatenate([blocks[s, here, :] for s in range(count // 2, count)], axis=1)
            full = jnp.concatenate([low, high], axis=1)

            def one_tile(j, unused):
                cols = pl.ds(pl.multiple_of(j * width, width), width)
                first = jnp.dot(low, sel_ref[:half, cols], preferred_element_type=jnp.float32)
                second = jnp.dot(low, sel_ref[half : 2 * half, cols], preferred_element_type=jnp.float32)
                third = jnp.dot(full, sel_ref[2 * half :, cols], preferred_element_type=jnp.float32)
                tile = (first * second * third).astype(jnp.bfloat16)
                tile_ref[here, cols] = tile
                sum_ref[...] += jnp.dot(tile, signs_ref[cols, :], preferred_element_type=jnp.float32)
                return unused

            lax.fori_loop(0, tiles, one_tile, 0, unroll=2)
            part_ref[here, :] = sum_ref[...].astype(jnp.bfloat16)

        @pl.when((base >= 1) & (base <= CHUNKS))
        def _():
            mine = rows_of(base - 1, me)
            total = part_ref[mine, :].astype(jnp.float32)
            for k in range(count - 1):
                reduce_copy(k, base - 1).wait_recv()
                total = total + slots[k, base - 1].astype(jnp.float32)
            full_ref[mine, :] = total.astype(jnp.bfloat16)

        return carry

    lax.fori_loop(0, CHUNKS + count + 1, one_round, 0)

    def drain(chunk, carry):
        for k in range(count - 1):
            spread_copy(k, chunk, lax.rem(me + count - 1 - k, count)).wait_recv()
            spread_copy(k, chunk, me).wait_send()
            reduce_copy(k, chunk).wait_send()
        for hop in range(count - 1):

            @pl.when((me >= hop) & (me < count - 1))
            def _():
                copy(0, hop, chunk, me - hop, me + 1).wait_send()

            @pl.when((me + hop < count) & (me > 0))
            def _():
                copy(1, hop, chunk, me + hop, me - 1).wait_send()

        return carry

    lax.fori_loop(0, CHUNKS, drain, 0)
    value_ref[...] = full_ref[...]


def gather_features(coeffs, triples, sketch, count):
    rows, part = coeffs.shape
    feats, rank = sketch.shape
    hops = max(count - 1, 1)
    step = rows // CHUNKS
    return pl.pallas_call(
        functools.partial(gather_kernel, count, min(512, feats)),
        in_specs=[VMEM] * 3,
        out_specs=[VMEM] * 2,
        out_shape=[
            jax.ShapeDtypeStruct((rows, feats), jnp.bfloat16),
            jax.ShapeDtypeStruct((rows, rank), jnp.bfloat16),
        ],
        scratch_shapes=[
            pltpu.VMEM((count, rows, part), jnp.bfloat16),
            pltpu.VMEM((2 * count * part, feats), jnp.bfloat16),
            pltpu.VMEM((feats, rank), jnp.bfloat16),
            pltpu.VMEM((step, rank), jnp.float32),
            pltpu.VMEM((rows, rank), jnp.bfloat16),
            pltpu.VMEM((hops, CHUNKS, step // count, rank), jnp.bfloat16),
            pltpu.VMEM((rows, rank), jnp.bfloat16),
            pltpu.SemaphoreType.DMA,
            pltpu.SemaphoreType.DMA((2, hops, CHUNKS)),
            pltpu.SemaphoreType.DMA((2, hops, CHUNKS)),
        ]
        + [pltpu.SemaphoreType.DMA((hops, CHUNKS))] * 4,
        compiler_params=pltpu.CompilerParams(
            collective_id=0, has_side_effects=True, vmem_limit_bytes=24 << 20
        ),
    )(coeffs, triples, sketch)


def peers_of(me, count):
    return [lax.rem(me + k, count) for k in range(1, count)]


def gram_kernel(count, width, value_ref, tile_ref, gram_ref, raw_ref, turned, slots, send_sem, recv_sem):
    me = lax.axis_index("img")
    peers = peers_of(me, count)
    turned[...] = value_ref[...].T
    slots[count - 1] = jnp.dot(turned[...], value_ref[...], preferred_element_type=jnp.float32)
    greet("img", peers)
    copies = []
    for k, peer in enumerate(peers):
        copies.append(
            pltpu.make_async_remote_copy(
                src_ref=slots.at[count - 1],
                dst_ref=slots.at[k],
                send_sem=send_sem.at[k],
                recv_sem=recv_sem.at[k],
                device_id={"img": peer},
                device_id_type=MESH,
            )
        )
        copies[-1].start()

    def one_tile(j, carry):
        cols = pl.ds(pl.multiple_of(j * width, width), width)
        raw_ref[:, cols] = jnp.dot(turned[...], tile_ref[:, cols], preferred_element_type=jnp.float32)
        return carry

    lax.fori_loop(0, tile_ref.shape[1] // width, one_tile, 0)
    for copy in copies:
        copy.wait_recv()
    total = jnp.zeros(gram_ref.shape, jnp.float32)
    for sender in range(count):
        total = total + slots[lax.rem(me + 2 * count - sender - 1, count)]
    gram_ref[...] = total
    for copy in copies:
        copy.wait_send()


def gram_and_raw(value, tiles, count):
    rows, rank = value.shape
    feats = tiles.shape[1]
    others = max(count - 1, 1)
    return pl.pallas_call(
        functools.partial(gram_kernel, count, min(512, feats)),
        in_specs=[VMEM] * 2,
        out_specs=[VMEM] * 2,
        out_shape=[
            jax.ShapeDtypeStruct((rank, rank), jnp.float32),
            jax.ShapeDtypeStruct((rank, feats), jnp.float32),
        ],
        scratch_shapes=[
            pltpu.VMEM((rank, rows), jnp.bfloat16),
            pltpu.VMEM((others + 1, rank, rank), jnp.float32),
            pltpu.SemaphoreType.DMA((others,)),
            pltpu.SemaphoreType.DMA((others,)),
        ],
        compiler_params=pltpu.CompilerParams(
            collective_id=2, has_side_effects=True, vmem_limit_bytes=16 << 20
        ),
    )(value, tiles)


def factor_kernel(scale, after, gram_ref, out_ref, left, right):
    size = gram_ref.shape[0]
    rows = lax.broadcasted_iota(jnp.int32, (size, size), 0)
    lanes = lax.broadcasted_iota(jnp.int32, (size, size), 1)
    left[...] = gram_ref[...] * scale
    right[...] = jnp.where(rows == lanes, 1.0, 0.0)

    def eliminate(j, carry):
        block = left[...]
        column = jnp.sum(jnp.where(lanes == j, block, 0.0), axis=1, keepdims=True)
        pivot_row = left[pl.ds(j, 1), :]
        pivot = jnp.sum(jnp.where(lanes[:1] == j, pivot_row, 0.0), axis=1, keepdims=True)
        factor = jnp.where(rows[:, :1] > j, column / pivot, 0.0)
        left[...] = block - factor * pivot_row
        right[...] = right[...] - factor * right[pl.ds(j, 1), :]
        return carry

    lax.fori_loop(0, size, eliminate, 0)
    diagonal = jnp.sum(jnp.where(rows == lanes, left[...], 0.0), axis=1, keepdims=True)
    out_ref[...] = right[...] * (after / jnp.sqrt(diagonal))


def inverse_factor(gram, scale, after):
    return pl.pallas_call(
        functools.partial(factor_kernel, scale, after),
        in_specs=[VMEM],
        out_specs=VMEM,
        out_shape=jax.ShapeDtypeStruct(gram.shape, jnp.float32),
        scratch_shapes=[pltpu.VMEM(gram.shape, jnp.float32)] * 2,
        compiler_params=pltpu.CompilerParams(vmem_limit_bytes=8 << 20),
    )(gram)


def rows_kernel(count, part_ref, out_ref, slots, send_sem, recv_sem):
    me = lax.axis_index("img")
    peers = peers_of(me, count)
    greet("img", peers)
    copies = []
    for k, peer in enumerate(peers):
        copies.append(
            pltpu.make_async_remote_copy(
                src_ref=part_ref.at[peer],
                dst_ref=slots.at[k],
                send_sem=send_sem.at[k],
                recv_sem=recv_sem.at[k],
                device_id={"img": peer},
                device_id_type=MESH,
            )
        )
        copies[-1].start()
    out_ref[...] = part_ref[me].astype(jnp.float32)
    for k, copy in enumerate(copies):
        copy.wait_recv()
        out_ref[...] += slots[k].astype(jnp.float32)
    for copy in copies:
        copy.wait_send()


def sum_rows(part, count):
    shape = part.shape[1:]
    others = max(count - 1, 1)
    return pl.pallas_call(
        functools.partial(rows_kernel, count),
        in_specs=[VMEM],
        out_specs=VMEM,
        out_shape=jax.ShapeDtypeStruct(shape, jnp.float32),
        scratch_shapes=[
            pltpu.VMEM((others,) + shape, part.dtype),
            pltpu.SemaphoreType.DMA((others,)),
            pltpu.SemaphoreType.DMA((others,)),
        ],
        compiler_params=pltpu.CompilerParams(collective_id=3, has_side_effects=True, vmem_limit_bytes=12 << 20),
    )(part)


def on_device(coeffs, triples, sketch):
    rows_here = coeffs.shape[0]
    feats_here = triples.shape[1]
    rank_cols = sketch.shape[1]
    img_count = lax.axis_size("img")
    feat_count = lax.axis_size("feat")
    total_rows = rows_here * img_count
    total_feats = feats_here * feat_count
    tiles, value = gather_features(coeffs, triples, sketch, feat_count)
    sketch_scale = (1.5 / total_feats) ** 0.5
    gram, raw = gram_and_raw(value, tiles, img_count)
    inverse = inverse_factor(gram, sketch_scale * sketch_scale / total_rows, sketch_scale)
    exact = lax.Precision.HIGHEST
    solved = jnp.dot(inverse, raw, precision=exact) / jnp.sqrt(jnp.float32(total_rows))
    outgoing = solved.astype(jnp.bfloat16).reshape(img_count, rank_cols // img_count, feats_here)
    projected = sum_rows(outgoing, img_count)
    basis = jnp.dot(value.astype(jnp.float32), inverse.T, precision=exact)
    return (basis, projected)


def solution(mesh):
    in_specs = (P("img", "feat"), P(None, "feat"), P("feat", None))
    out_specs = (P("img", None), P("img", "feat"))
    return jax.shard_map(
        on_device, mesh=mesh, in_specs=in_specs, out_specs=out_specs, check_vma=False
    )
```

profile of v0, /device:TPU:0, one launch (start us, length us, event | category | flops | bytes accessed | tf_op | source)
XLA Modules:
  0.0 115.9 jit_solution(9839418782644381346)
XLA Ops:
  0.6 0.0 copy-start
  0.6 1.6 %copy-done = s32[4096,128]{1,0:T(8,128)S(1)} copy-done((s32[4096,128]{1,0:T(8,128)S(1)}, s32[4096,128]{1,0:T(8,128)}, u32[]{:S(2)}) %copy-start) | copy-done | bytes 2097176
  2.2 0.0 copy-start.1
  2.2 1.0 copy-done.1
  3.3 0.0 copy-start.2
  3.3 0.8 copy-done.2
  4.1 70.4 %shard_map.50 = (bf16[2048,4096]{1,0:T(8,128)(2,1)S(1)}, bf16[2048,128]{1,0:T(8,128)(2,1)S(1)}) custom-call(bf16[2048,128]{1,0:T(8,128)(2,1)S(1)} %copy-done.1, s32[3,4096]{1,0:T(4,128)S(1)} %copy-done.2, s32[4096,128]{1,0:T(8,128)S(1)} %copy-done), custom_call_target="tpu_custom_call" | custom-call | tf_op jit(solution)/shard_map/pallas_call | solution.py:192
  74.5 9.3 %shard_map.51 = (f32[128,128]{1,0:T(8,128)S(1)}, f32[128,4096]{1,0:T(8,128)S(1)}) custom-call(bf16[2048,128]{1,0:T(8,128)(2,1)S(1)} %get-tuple-element.6.value_ref, bf16[2048,4096]{1,0:T(8,128)(2,1)S(1)} %get-tuple-element.7.tile_ref), custom_call_target="tpu_custom_call" | custom-call | tf_op jit(solution)/shard_map/pallas_call | solution.py:263
  83.8 13.4 %shard_map.52 = f32[128,128]{1,0:T(8,128)S(1)} custom-call(f32[128,128]{1,0:T(8,128)S(1)} %get-tuple-element.8.gram_ref), custom_call_target="tpu_custom_call" | custom-call | tf_op jit(solution)/shard_map/pallas_call | solution.py:306
  97.3 1.9 %fusion = bf16[128,4096]{1,0:T(8,128)(2,1)S(1)} fusion(f32[128,128]{1,0:T(8,128)S(1)} %shard_map.52, f32[128,4096]{1,0:T(8,128)S(1)} %get-tuple-element.9), kind=kOutput, calls=%fused_computation.1 | convolution fusion | flops 806354944 | bytes 3211264 | tf_op jit(solution)/shard_map/dot_general | solution.py:371
  99.2 14.5 %shard_map.53 = f32[16,4096]{1,0:T(8,128)S(1)} custom-call(bf16[8,16,4096]{2,1,0:T(8,128)(2,1)S(1)} %bitcast.5), custom_call_target="tpu_custom_call" | custom-call | tf_op jit(solution)/shard_map/pallas_call | solution.py:344
  113.7 1.6 %fusion.1 = f32[2048,128]{1,0:T(8,128)} fusion(bf16[2048,128]{1,0:T(8,128)(2,1)S(1)} %get-tuple-element.6.value_ref, f32[128,128]{1,0:T(8,128)S(1)} %shard_map.52), kind=kOutput, calls=%fused_computation.2 | convolution fusion | flops 402653184 | bytes 1638400 | tf_op jit(solution)/shard_map/dot_general | solution.py:374
  115.2 0.7 copy.6
Async XLA Ops:
  0.6 1.6 %copy-start = (s32[4096,128]{1,0:T(8,128)S(1)}, s32[4096,128]{1,0:T(8,128)}, u32[]{:S(2)}) copy-start(s32[4096,128]{1,0:T(8,128)} %sketch_ref.1) | copy-start | bytes 6291460
  2.2 1.0 copy-start.1
  3.3 0.8 copy-start.2
where the time goes:
time: 117 us; the launch traced here: 116 us
  Pallas kernels  108 us (92%)
  local copies, waits for them, and re-layouts  4.17 us (4%)
  matrix products  3.48 us (3%)
    pallas_call x1, Pallas kernels, gather_features(): pl.pallas_call(functools.partial(gather_kernel, count, min(512, feats)),...  70.4 us
    pallas_call x1, Pallas kernels, sum_rows(): pl.pallas_call(functools.partial(rows_kernel, count), in_specs=[VMEM], ou...  14.5 us
    pallas_call x1, Pallas kernels, inverse_factor(): pl.pallas_call(functools.partial(factor_kernel, scale, after), in_specs=[...  13.4 us
    pallas_call x1, Pallas kernels, gram_and_raw(): pl.pallas_call(functools.partial(gram_kernel, count, min(512, feats)), in...  9.32 us
    unnamed x7, local copies, waits for them, and re-layouts  4.17 us

commit v1 on v0

--- a/solution.py
+++ b/solution.py
@@ -220,158 +220,156 @@
     return [lax.rem(me + k, count) for k in range(1, count)]
 
 
-def gram_kernel(count, width, value_ref, tile_ref, gram_ref, raw_ref, turned, slots, send_sem, recv_sem):
+def factor_panels(scale, after, gram, left, right, pivots, out_ref, width):
+    size = gram.shape[0]
+    rows = lax.broadcasted_iota(jnp.int32, (width, size), 0)
+    lanes = lax.broadcasted_iota(jnp.int32, (width, size), 1)
+    left[...] = gram * scale
+    whole_rows = lax.broadcasted_iota(jnp.int32, (size, size), 0)
+    whole_lanes = lax.broadcasted_iota(jnp.int32, (size, size), 1)
+    right[...] = jnp.where(whole_rows == whole_lanes, 1.0, 0.0)
+
+    def panel(p, carry):
+        first = pl.multiple_of(p * width, width)
+        here = pl.ds(first, width)
+        block = left[here, :]
+        twin = right[here, :]
+        inverse = jnp.zeros((width, size), jnp.float32)
+        kept = jnp.zeros((width, size), jnp.float32)
+        for j in range(width):
+            column = jnp.take_along_axis(block, jnp.full((width, size), first + j, jnp.int32), axis=1)
+            pivot = column[j : j + 1, :]
+            ratio = 1.0 / pivot
+            inverse = jnp.where(rows == j, ratio, inverse)
+            kept = jnp.where(rows == j, pivot, kept)
+            if j + 1 < width:
+                factor = jnp.where(rows > j, column * ratio, 0.0)
+                block = block - factor * block[j : j + 1, :]
+                twin = twin - factor * twin[j : j + 1, :]
+        pivots[here, :] = kept
+        right[here, :] = twin
+
+        @pl.when(p + 1 < size // width)
+        def _():
+            factor = jnp.where(lanes >= first + width, block * inverse, 0.0)
+            across = (((0,), (0,)), ((), ()))
+            exact = lax.Precision.HIGHEST
+            left[...] -= lax.dot_general(factor, block, across, precision=exact, preferred_element_type=jnp.float32)
+            right[...] -= lax.dot_general(factor, twin, across, precision=exact, preferred_element_type=jnp.float32)
+
+        return carry
+
+    lax.fori_loop(0, size // width, panel, 0)
+    out_ref[...] = right[...] * (after / jnp.sqrt(pivots[...]))
+
+
+def finish_kernel(
+    count, scale, after, root, value_ref, tile_ref, inverse_ref, out_ref, turned, gram_slots, staged, raw_slots,
+    solved_ref, row_slots, left, right, pivots, gram_send, gram_recv, raw_send, raw_recv, row_send, row_recv
+):
     me = lax.axis_index("img")
     peers = peers_of(me, count)
+    others = count - 1
+    span = tile_ref.shape[1] // count
+    part = out_ref.shape[0]
+
+    def columns(owner):
+        return pl.ds(pl.multiple_of(owner * span, span), span)
+
+    def remote(source, target, send, recv, k):
+        return pltpu.make_async_remote_copy(
+            src_ref=source,
+            dst_ref=target,
+            send_sem=send.at[k],
+            recv_sem=recv.at[k],
+            device_id={"img": peers[k]},
+            device_id_type=MESH,
+        )
+
     turned[...] = value_ref[...].T
-    slots[count - 1] = jnp.dot(turned[...], value_ref[...], preferred_element_type=jnp.float32)
+    gram_slots[others] = jnp.dot(turned[...], value_ref[...], preferred_element_type=jnp.float32)
     greet("img", peers)
-    copies = []
-    for k, peer in enumerate(peers):
-        copies.append(
-            pltpu.make_async_remote_copy(
-                src_ref=slots.at[count - 1],
-                dst_ref=slots.at[k],
-                send_sem=send_sem.at[k],
-                recv_sem=recv_sem.at[k],
-                device_id={"img": peer},
-                device_id_type=MESH,
-            )
-        )
-        copies[-1].start()
-
-    def one_tile(j, carry):
-        cols = pl.ds(pl.multiple_of(j * width, width), width)
-        raw_ref[:, cols] = jnp.dot(turned[...], tile_ref[:, cols], preferred_element_type=jnp.float32)
-        return carry
-
-    lax.fori_loop(0, tile_ref.shape[1] // width, one_tile, 0)
-    for copy in copies:
+    grams = [remote(gram_slots.at[others], gram_slots.at[k], gram_send, gram_recv, k) for k in range(others)]
+    raws = [remote(staged.at[k], raw_slots.at[k], raw_send, raw_recv, k) for k in range(others)]
+    sends = [
+        remote(solved_ref.at[pl.ds(pl.multiple_of(peers[k] * part, part), part)], row_slots.at[k], row_send, row_recv, k)
+        for k in range(others)
+    ]
+    for copy in grams:
+        copy.start()
+    for k in range(others):
+        raw = jnp.dot(turned[...], tile_ref[:, columns(peers[k])], preferred_element_type=jnp.float32)
+        staged[k] = raw.astype(jnp.bfloat16)
+        raws[k].start()
+    mine = jnp.dot(turned[...], tile_ref[:, columns(me)], preferred_element_type=jnp.float32)
+    for copy in grams:
         copy.wait_recv()
-    total = jnp.zeros(gram_ref.shape, jnp.float32)
+    total = jnp.zeros(inverse_ref.shape, jnp.float32)
     for sender in range(count):
-        total = total + slots[lax.rem(me + 2 * count - sender - 1, count)]
-    gram_ref[...] = total
-    for copy in copies:
+        total = total + gram_slots[lax.rem(me + 2 * count - sender - 1, count)]
+    factor_panels(scale, after, total, left, right, pivots, inverse_ref, min(32, total.shape[0]))
+    for k, copy in enumerate(raws):
+        copy.wait_recv()
+        mine = mine + raw_slots[k].astype(jnp.float32)
+    solved = jnp.dot(inverse_ref[...], mine, precision=lax.Precision.HIGHEST, preferred_element_type=jnp.float32) * root
+    solved_ref[...] = solved.astype(jnp.bfloat16)
+    for copy in sends:
+        copy.start()
+    out_ref[:, columns(me)] = solved_ref[pl.ds(pl.multiple_of(me * part, part), part), :].astype(jnp.float32)
+    for k, copy in enumerate(sends):
+        copy.wait_recv()
+        sender = lax.rem(me + count - 1 - k, count)
+        out_ref[:, columns(sender)] = row_slots[k].astype(jnp.float32)
+    for copy in grams + raws + sends:
         copy.wait_send()
 
 
-def gram_and_raw(value, tiles, count):
+def finish(value, tiles, count, scale, after, root):
     rows, rank = value.shape
     feats = tiles.shape[1]
     others = max(count - 1, 1)
+    span = feats // count
+    part = rank // count
+    square = pltpu.VMEM((rank, rank), jnp.float32)
     return pl.pallas_call(
-        functools.partial(gram_kernel, count, min(512, feats)),
+        functools.partial(finish_kernel, count, scale, after, root),
         in_specs=[VMEM] * 2,
         out_specs=[VMEM] * 2,
         out_shape=[
             jax.ShapeDtypeStruct((rank, rank), jnp.float32),
-            jax.ShapeDtypeStruct((rank, feats), jnp.float32),
+            jax.ShapeDtypeStruct((part, feats), jnp.float32),
         ],
         scratch_shapes=[
             pltpu.VMEM((rank, rows), jnp.bfloat16),
             pltpu.VMEM((others + 1, rank, rank), jnp.float32),
-            pltpu.SemaphoreType.DMA((others,)),
-            pltpu.SemaphoreType.DMA((others,)),
-        ],
+            pltpu.VMEM((others, rank, span), jnp.bfloat16),
+            pltpu.VMEM((others, rank, span), jnp.bfloat16),
+            pltpu.VMEM((rank, span), jnp.bfloat16),
+            pltpu.VMEM((others, part, span), jnp.bfloat16),
+            square,
+            square,
+            square,
+        ]
+        + [pltpu.SemaphoreType.DMA((others,))] * 6,
         compiler_params=pltpu.CompilerParams(
-            collective_id=2, has_side_effects=True, vmem_limit_bytes=16 << 20
+            collective_id=2, has_side_effects=True, vmem_limit_bytes=20 << 20
         ),
     )(value, tiles)
-
-
-def factor_kernel(scale, after, gram_ref, out_ref, left, right):
-    size = gram_ref.shape[0]
-    rows = lax.broadcasted_iota(jnp.int32, (size, size), 0)
-    lanes = lax.broadcasted_iota(jnp.int32, (size, size), 1)
-    left[...] = gram_ref[...] * scale
-    right[...] = jnp.where(rows == lanes, 1.0, 0.0)
-
-    def eliminate(j, carry):
-        block = left[...]
-        column = jnp.sum(jnp.where(lanes == j, block, 0.0), axis=1, keepdims=True)
-        pivot_row = left[pl.ds(j, 1), :]
-        pivot = jnp.sum(jnp.where(lanes[:1] == j, pivot_row, 0.0), axis=1, keepdims=True)
-        factor = jnp.where(rows[:, :1] > j, column / pivot, 0.0)
-        left[...] = block - factor * pivot_row
-        right[...] = right[...] - factor * right[pl.ds(j, 1), :]
-        return carry
-
-    lax.fori_loop(0, size, eliminate, 0)
-    diagonal = jnp.sum(jnp.where(rows == lanes, left[...], 0.0), axis=1, keepdims=True)
-    out_ref[...] = right[...] * (after / jnp.sqrt(diagonal))
-
-
-def inverse_factor(gram, scale, after):
-    return pl.pallas_call(
-        functools.partial(factor_kernel, scale, after),
-        in_specs=[VMEM],
-        out_specs=VMEM,
-        out_shape=jax.ShapeDtypeStruct(gram.shape, jnp.float32),
-        scratch_shapes=[pltpu.VMEM(gram.shape, jnp.float32)] * 2,
-        compiler_params=pltpu.CompilerParams(vmem_limit_bytes=8 << 20),
-    )(gram)
-
-
-def rows_kernel(count, part_ref, out_ref, slots, send_sem, recv_sem):
-    me = lax.axis_index("img")
-    peers = peers_of(me, count)
-    greet("img", peers)
-    copies = []
-    for k, peer in enumerate(peers):
-        copies.append(
-            pltpu.make_async_remote_copy(
-                src_ref=part_ref.at[peer],
-                dst_ref=slots.at[k],
-                send_sem=send_sem.at[k],
-                recv_sem=recv_sem.at[k],
-                device_id={"img": peer},
-                device_id_type=MESH,
-            )
-        )
-        copies[-1].start()
-    out_ref[...] = part_ref[me].astype(jnp.float32)
-    for k, copy in enumerate(copies):
-        copy.wait_recv()
-        out_ref[...] += slots[k].astype(jnp.float32)
-    for copy in copies:
-        copy.wait_send()
-
-
-def sum_rows(part, count):
-    shape = part.shape[1:]
-    others = max(count - 1, 1)
-    return pl.pallas_call(
-        functools.partial(rows_kernel, count),
-        in_specs=[VMEM],
-        out_specs=VMEM,
-        out_shape=jax.ShapeDtypeStruct(shape, jnp.float32),
-        scratch_shapes=[
-            pltpu.VMEM((others,) + shape, part.dtype),
-            pltpu.SemaphoreType.DMA((others,)),
-            pltpu.SemaphoreType.DMA((others,)),
-        ],
-        compiler_params=pltpu.CompilerParams(collective_id=3, has_side_effects=True, vmem_limit_bytes=12 << 20),
-    )(part)
 
 
 def on_device(coeffs, triples, sketch):
     rows_here = coeffs.shape[0]
     feats_here = triples.shape[1]
-    rank_cols = sketch.shape[1]
     img_count = lax.axis_size("img")
     feat_count = lax.axis_size("feat")
     total_rows = rows_here * img_count
     total_feats = feats_here * feat_count
     tiles, value = gather_features(coeffs, triples, sketch, feat_count)
     sketch_scale = (1.5 / total_feats) ** 0.5
-    gram, raw = gram_and_raw(value, tiles, img_count)
-    inverse = inverse_factor(gram, sketch_scale * sketch_scale / total_rows, sketch_scale)
-    exact = lax.Precision.HIGHEST
-    solved = jnp.dot(inverse, raw, precision=exact) / jnp.sqrt(jnp.float32(total_rows))
-    outgoing = solved.astype(jnp.bfloat16).reshape(img_count, rank_cols // img_count, feats_here)
-    projected = sum_rows(outgoing, img_count)
-    basis = jnp.dot(value.astype(jnp.float32), inverse.T, precision=exact)
+    inverse, projected = finish(
+        value, tiles, img_count, sketch_scale * sketch_scale / total_rows, sketch_scale, total_rows**-0.5
+    )
+    basis = jnp.dot(value.astype(jnp.float32), inverse.T, precision=lax.Precision.HIGHEST)
     return (basis, projected)
 
 

time: 117 us -> 104 us (0.89)
  Pallas kernels: 108 us -> 97.2 us
  matrix products: 3.48 us -> 1.57 us
    pallas_call x3 -> x1, Pallas kernels: 37.2 us -> 26.9 us  [finish(): pl.pallas_call(functools.partial(finish_kernel, count, scale, after, root...]
    dot_general x2 -> x1, matrix products: 3.48 us -> 1.57 us  [on_device(): jnp.dot(value.astype(jnp.float32), inverse.T, precision=lax.Precision.HIG...]
where the time goes in v1:
time: 104 us
  Pallas kernels  97.2 us (93%)
  local copies, waits for them, and re-layouts  4.17 us (4%)
  matrix products  1.57 us (2%)
    pallas_call x1, Pallas kernels, gather_features(): pl.pallas_call(functools.partial(gather_kernel, count, min(512, feats)),...  70.4 us
    pallas_call x1, Pallas kernels, finish(): pl.pallas_call(functools.partial(finish_kernel, count, scale, after, root...  26.9 us
    unnamed x7, local copies, waits for them, and re-layouts  4.17 us

profile of v1, /device:TPU:0, one launch (start us, length us, event | category | flops | bytes accessed | tf_op | source)
XLA Modules:
  0.0 103.6 jit_solution(2202432526777320546)
XLA Ops:
  0.6 0.0 copy-start
  0.6 1.6 %copy-done = s32[4096,128]{1,0:T(8,128)S(1)} copy-done((s32[4096,128]{1,0:T(8,128)S(1)}, s32[4096,128]{1,0:T(8,128)}, u32[]{:S(2)}) %copy-start) | copy-done | bytes 2097176
  2.2 0.0 copy-start.1
  2.2 1.0 %copy-done.1 = bf16[2048,128]{1,0:T(8,128)(2,1)S(1)} copy-done((bf16[2048,128]{1,0:T(8,128)(2,1)S(1)}, bf16[2048,128]{1,0:T(8,128)(2,1)}, u32[]{:S(2)}) %copy-start.1) | copy-done | bytes 524312
  3.3 0.0 copy-start.2
  3.3 0.8 copy-done.2
  4.1 70.4 %shard_map.50 = (bf16[2048,4096]{1,0:T(8,128)(2,1)S(1)}, bf16[2048,128]{1,0:T(8,128)(2,1)S(1)}) custom-call(bf16[2048,128]{1,0:T(8,128)(2,1)S(1)} %copy-done.1, s32[3,4096]{1,0:T(4,128)S(1)} %copy-done.2, s32[4096,128]{1,0:T(8,128)S(1)} %copy-done), custom_call_target="tpu_custom_call" | custom-call | tf_op jit(solution)/shard_map/pallas_call | solution.py:192
  74.5 26.9 %shard_map.51 = (f32[128,128]{1,0:T(8,128)S(1)}, f32[16,4096]{1,0:T(8,128)S(1)}) custom-call(bf16[2048,128]{1,0:T(8,128)(2,1)S(1)} %get-tuple-element.6.value_ref, bf16[2048,4096]{1,0:T(8,128)(2,1)S(1)} %get-tuple-element.7.tile_ref), custom_call_target="tpu_custom_call" | custom-call | tf_op jit(solution)/shard_map/pallas_call | solution.py:334
  101.4 1.6 %fusion = f32[2048,128]{1,0:T(8,128)} fusion(bf16[2048,128]{1,0:T(8,128)(2,1)S(1)} %get-tuple-element.6.value_ref, f32[128,128]{1,0:T(8,128)S(1)} %get-tuple-element.8), kind=kOutput, calls=%fused_computation | convolution fusion | flops 402653184 | bytes 1638400 | tf_op jit(solution)/shard_map/dot_general | solution.py:372
  102.9 0.7 copy.6
Async XLA Ops:
  0.6 1.6 %copy-start = (s32[4096,128]{1,0:T(8,128)S(1)}, s32[4096,128]{1,0:T(8,128)}, u32[]{:S(2)}) copy-start(s32[4096,128]{1,0:T(8,128)} %sketch_ref.1) | copy-start | bytes 6291460
  2.2 1.0 %copy-start.1 = (bf16[2048,128]{1,0:T(8,128)(2,1)S(1)}, bf16[2048,128]{1,0:T(8,128)(2,1)}, u32[]{:S(2)}) copy-start(bf16[2048,128]{1,0:T(8,128)(2,1)} %coeffs_ref.1) | copy-start | bytes 1572868
  3.3 0.8 copy-start.2

commit v2 on v1

--- a/solution.py
+++ b/solution.py
@@ -8,8 +8,11 @@
 from jax.sharding import PartitionSpec as P
 
 CHUNKS = 8
+AHEAD = 2
+SUB = 8
 MESH = pl.DeviceIdType.MESH
 VMEM = pl.BlockSpec(memory_space=pltpu.VMEM)
+HBM = pl.BlockSpec(memory_space=pltpu.HBM)
 
 
 def greet(axis, peers):
@@ -20,11 +23,11 @@
 
 
 def gather_kernel(
-    count, width, coeffs_ref, triples_ref, sketch_ref, tile_ref, value_ref, blocks, sel_ref, signs_ref,
-    sum_ref, part_ref, slots, full_ref, own_sem, send_sem, recv_sem, to_sem, from_sem, out_sem, in_sem
+    count, width, coeffs_hbm, triples_hbm, sketch_hbm, tile_ref, value_ref, triples_ref, sketch_ref, blocks, sel_ref,
+    signs_ref, sum_ref, part_ref, slots, full_ref, own_sem, send_sem, recv_sem, to_sem, from_sem, out_sem, in_sem
 ):
     me = lax.axis_index("feat")
-    rows, part = coeffs_ref.shape
+    rows, part = coeffs_hbm.shape
     step = rows // CHUNKS
     half = count * part // 2
     tiles = sketch_ref.shape[0] // width
@@ -38,18 +41,23 @@
             levels = lax.broadcasted_iota(jnp.int32, (depth, width), 0)
             chosen = triples_ref[index : index + 1, cols]
             sel_ref[start : start + depth, cols] = jnp.where(levels == chosen, 1.0, 0.0).astype(jnp.bfloat16)
-            if index == 0:
+            if index == 2:
                 signs_ref[cols, :] = sketch_ref[cols, :].astype(jnp.float32).astype(jnp.bfloat16)
             return carry
 
         lax.fori_loop(0, tiles, one, 0)
 
-    own = pltpu.make_async_copy(coeffs_ref, blocks.at[me], own_sem)
+    own = pltpu.make_async_copy(coeffs_hbm, blocks.at[me], own_sem.at[0])
     own.start()
+    triples_copy = pltpu.make_async_copy(triples_hbm, triples_ref, own_sem.at[1])
+    triples_copy.start()
+    sketch_copy = pltpu.make_async_copy(sketch_hbm, sketch_ref, own_sem.at[2])
+    sketch_copy.start()
     peers = peers_of(me, count)
     piece = step // count
     greet("feat", peers)
     own.wait()
+    triples_copy.wait()
 
     def copy(side, hop, chunk, source, target):
         span = blocks.at[source, pl.ds(pl.multiple_of(chunk * step, step), step)]
@@ -86,6 +94,18 @@
             device_id_type=MESH,
         )
 
+    def send_own(chunk, live):
+        @pl.when(live & (me < count - 1))
+        def _():
+            copy(0, 0, chunk, me, me + 1).start()
+
+        @pl.when(live & (me > 0))
+        def _():
+            copy(1, 0, chunk, me, me - 1).start()
+
+    for chunk in range(AHEAD):
+        send_own(chunk, True)
+
     def one_round(turn, carry):
         for hop in range(count):
             chunk = turn - hop
@@ -100,7 +120,7 @@
                 def _():
                     copy(1, hop - 1, chunk, me + hop, me + 1).wait_recv()
 
-            if hop < count - 1:
+            if 0 < hop < count - 1:
 
                 @pl.when(live & (me >= hop) & (me < count - 1))
                 def _():
@@ -110,10 +130,14 @@
                 def _():
                     copy(1, hop, chunk, me + hop, me - 1).start()
 
+        send_own(turn + AHEAD, (turn + AHEAD) < CHUNKS)
+
         for index in range(3):
 
             @pl.when(turn == min(index, count - 2))
             def _():
+                if index == 2:
+                    sketch_copy.wait()
                 build(index)
 
         base = turn - (count - 1)
@@ -190,14 +214,16 @@
     hops = max(count - 1, 1)
     step = rows // CHUNKS
     return pl.pallas_call(
-        functools.partial(gather_kernel, count, min(512, feats)),
-        in_specs=[VMEM] * 3,
+        functools.partial(gather_kernel, count, min(1024, feats)),
+        in_specs=[HBM] * 3,
         out_specs=[VMEM] * 2,
         out_shape=[
             jax.ShapeDtypeStruct((rows, feats), jnp.bfloat16),
             jax.ShapeDtypeStruct((rows, rank), jnp.bfloat16),
         ],
         scratch_shapes=[
+            pltpu.VMEM(triples.shape, jnp.int32),
+            pltpu.VMEM((feats, rank), jnp.int32),
             pltpu.VMEM((count, rows, part), jnp.bfloat16),
             pltpu.VMEM((2 * count * part, feats), jnp.bfloat16),
             pltpu.VMEM((feats, rank), jnp.bfloat16),
@@ -205,7 +231,7 @@
             pltpu.VMEM((rows, rank), jnp.bfloat16),
             pltpu.VMEM((hops, CHUNKS, step // count, rank), jnp.bfloat16),
             pltpu.VMEM((rows, rank), jnp.bfloat16),
-            pltpu.SemaphoreType.DMA,
+            pltpu.SemaphoreType.DMA((3,)),
             pltpu.SemaphoreType.DMA((2, hops, CHUNKS)),
             pltpu.SemaphoreType.DMA((2, hops, CHUNKS)),
         ]
@@ -213,7 +239,7 @@
         compiler_params=pltpu.CompilerParams(
             collective_id=0, has_side_effects=True, vmem_limit_bytes=24 << 20
         ),
-    )(coeffs, triples, sketch)
+    )(*(pltpu.with_memory_space_constraint(a, pltpu.HBM) for a in (coeffs, triples, sketch)))
 
 
 def peers_of(me, count):
@@ -235,18 +261,22 @@
         block = left[here, :]
         twin = right[here, :]
         inverse = jnp.zeros((width, size), jnp.float32)
-        kept = jnp.zeros((width, size), jnp.float32)
-        for j in range(width):
-            column = jnp.take_along_axis(block, jnp.full((width, size), first + j, jnp.int32), axis=1)
-            pivot = column[j : j + 1, :]
-            ratio = 1.0 / pivot
-            inverse = jnp.where(rows == j, ratio, inverse)
-            kept = jnp.where(rows == j, pivot, kept)
-            if j + 1 < width:
-                factor = jnp.where(rows > j, column * ratio, 0.0)
-                block = block - factor * block[j : j + 1, :]
-                twin = twin - factor * twin[j : j + 1, :]
-        pivots[here, :] = kept
+        for start in range(0, width, SUB):
+            columns = [
+                jnp.take_along_axis(block, jnp.full((width, size), first + start + j, jnp.int32), axis=1)
+                for j in range(SUB)
+            ]
+            for j in range(SUB):
+                at = start + j
+                ratio = 1.0 / columns[j][at : at + 1, :]
+                inverse = jnp.where(rows == at, ratio, inverse)
+                if at + 1 < width:
+                    factor = jnp.where(rows > at, columns[j] * ratio, 0.0)
+                    for m in range(j + 1, SUB):
+                        columns[m] = columns[m] - factor * columns[m][at : at + 1, :]
+                    block = block - factor * block[at : at + 1, :]
+                    twin = twin - factor * twin[at : at + 1, :]
+        pivots[here, :] = inverse
         right[here, :] = twin
 
         @pl.when(p + 1 < size // width)
@@ -260,7 +290,7 @@
         return carry
 
     lax.fori_loop(0, size // width, panel, 0)
-    out_ref[...] = right[...] * (after / jnp.sqrt(pivots[...]))
+    out_ref[...] = right[...] * (after * jnp.sqrt(pivots[...]))
 
 
 def finish_kernel(
@@ -352,7 +382,7 @@
         ]
         + [pltpu.SemaphoreType.DMA((others,))] * 6,
         compiler_params=pltpu.CompilerParams(
-            collective_id=2, has_side_effects=True, vmem_limit_bytes=20 << 20
+            collective_id=2, has_side_effects=True, vmem_limit_bytes=12 << 20
         ),
     )(value, tiles)
 

time: 104 us -> 94.7 us (0.911)
  Pallas kernels: 97.2 us -> 91.7 us
  local copies, waits for them, and re-layouts: 4.17 us -> 0.7 us
    pallas_call x1, Pallas kernels: 70.4 us -> 66.4 us  [gather_features(): pl.pallas_call(functools.partial(gather_kernel, count, min(1024, feats)),...]
    unnamed x7 -> x1, local copies, waits for them, and re-layouts: 4.17 us -> 0.7 us
    pallas_call x1, Pallas kernels: 26.9 us -> 25.3 us  [finish(): pl.pallas_call(functools.partial(finish_kernel, count, scale, after, root...]
where the time goes in v2:
time: 94.7 us; the launch traced here: 94.6 us
  Pallas kernels  91.7 us (97%)
  matrix products  1.57 us (2%)
    pallas_call x1, Pallas kernels, gather_features(): pl.pallas_call(functools.partial(gather_kernel, count, min(1024, feats)),...  66.4 us
    pallas_call x1, Pallas kernels, finish(): pl.pallas_call(functools.partial(finish_kernel, count, scale, after, root...  25.3 us

profile of v2, /device:TPU:0, one launch (start us, length us, event | category | flops | bytes accessed | tf_op | source)
XLA Modules:
  0.0 94.6 jit_solution(14901792180969284272)
XLA Ops:
  0.6 66.4 %shard_map.50 = (bf16[2048,4096]{1,0:T(8,128)(2,1)S(1)}, bf16[2048,128]{1,0:T(8,128)(2,1)S(1)}) custom-call(bf16[2048,128]{1,0:T(8,128)(2,1)} %coeffs_hbm.1, s32[3,4096]{1,0:T(4,128)} %triples_hbm.1, s32[4096,128]{1,0:T(8,128)} %sketch_hbm.1), custom_call_target="tpu_custom_call" | custom-call | tf_op jit(solution)/shard_map/pallas_call | solution.py:216
  67.1 25.3 %shard_map.51 = (f32[128,128]{1,0:T(8,128)S(1)}, f32[16,4096]{1,0:T(8,128)S(1)}) custom-call(bf16[2048,128]{1,0:T(8,128)(2,1)S(1)} %get-tuple-element.6.value_ref, bf16[2048,4096]{1,0:T(8,128)(2,1)S(1)} %get-tuple-element.7.tile_ref), custom_call_target="tpu_custom_call" | custom-call | tf_op jit(solution)/shard_map/pallas_call | solution.py:364
  92.3 1.6 %fusion = f32[2048,128]{1,0:T(8,128)} fusion(bf16[2048,128]{1,0:T(8,128)(2,1)S(1)} %get-tuple-element.6.value_ref, f32[128,128]{1,0:T(8,128)S(1)} %get-tuple-element.8), kind=kOutput, calls=%fused_computation | convolution fusion | flops 402653184 | bytes 1638400 | tf_op jit(solution)/shard_map/dot_general | solution.py:402
  93.9 0.7 copy.6

commit v3 on v0

v3 whole, which is shorter than its diff:
```python
import functools

import jax
import jax.numpy as jnp
from jax import lax
from jax.experimental import pallas as pl
from jax.experimental.pallas import tpu as pltpu
from jax.sharding import PartitionSpec as P

CHUNKS = 8
AHEAD = 2
SUB = 8
PANEL = 32
MESH = pl.DeviceIdType.MESH
VMEM = pl.BlockSpec(memory_space=pltpu.VMEM)
HBM = pl.BlockSpec(memory_space=pltpu.HBM)


def greet(groups):
    barrier = pltpu.get_barrier_semaphore()
    for axis, peers in groups:
        for peer in peers:
            pl.semaphore_signal(barrier, inc=1, device_id={axis: peer}, device_id_type=MESH)
    pl.semaphore_wait(barrier, sum(len(peers) for axis, peers in groups))


def peers_of(me, count):
    return [lax.rem(me + k, count) for k in range(1, count)]


def factor_panels(scale, after, gram, left, right, pivots, out_ref, width):
    size = gram.shape[0]
    rows = lax.broadcasted_iota(jnp.int32, (width, size), 0)
    lanes = lax.broadcasted_iota(jnp.int32, (width, size), 1)
    left[...] = gram * scale
    whole_rows = lax.broadcasted_iota(jnp.int32, (size, size), 0)
    whole_lanes = lax.broadcasted_iota(jnp.int32, (size, size), 1)
    right[...] = jnp.where(whole_rows == whole_lanes, 1.0, 0.0)

    def panel(p, carry):
        first = pl.multiple_of(p * width, width)
        here = pl.ds(first, width)
        block = left[here, :]
        twin = right[here, :]
        inverse = jnp.zeros((width, size), jnp.float32)
        for start in range(0, width, SUB):
            columns = [
                jnp.take_along_axis(block, jnp.full((width, size), first + start + j, jnp.int32), axis=1)
                for j in range(SUB)
            ]
            for j in range(SUB):
                at = start + j
                ratio = 1.0 / columns[j][at : at + 1, :]
                inverse = jnp.where(rows == at, ratio, inverse)
                if at + 1 < width:
                    factor = jnp.where(rows > at, columns[j] * ratio, 0.0)
                    for m in range(j + 1, SUB):
                        columns[m] = columns[m] - factor * columns[m][at : at + 1, :]
                    block = block - factor * block[at : at + 1, :]
                    twin = twin - factor * twin[at : at + 1, :]
        pivots[here, :] = inverse
        right[here, :] = twin

        @pl.when(p + 1 < size // width)
        def _():
            factor = jnp.where(lanes >= first + width, block * inverse, 0.0)
            across = (((0,), (0,)), ((), ()))
            exact = lax.Precision.HIGHEST
            left[...] -= lax.dot_general(factor, block, across, precision=exact, preferred_element_type=jnp.float32)
            right[...] -= lax.dot_general(factor, twin, across, precision=exact, preferred_element_type=jnp.float32)

        return carry

    lax.fori_loop(0, size // width, panel, 0)
    out_ref[...] = right[...] * (after * jnp.sqrt(pivots[...]))


def whole_kernel(
    count, images, width, scale, after, root, coeffs_hbm, triples_hbm, sketch_hbm, value_ref, inverse_ref, out_ref,
    triples_ref, sketch_ref, tile_ref, blocks, sel_ref, signs_ref, sum_ref, part_ref, slots, full_ref, gram_ref,
    raw_ref, pair_gram, chip_gram, pair_staged, pair_raw, chip_staged, chip_raw, solved_ref, row_slots, left, right,
    pivots, own_sem, send_sem, recv_sem, to_sem, from_sem, out_sem, in_sem, gram_send, gram_recv, pair_send, pair_recv,
    chip_send, chip_recv, row_send, row_recv
):
    me = lax.axis_index("feat")
    spot = lax.axis_index("img")
    rows, part = coeffs_hbm.shape
    feats = triples_ref.shape[1]
    step = rows // CHUNKS
    half = count * part // 2
    tiles = feats // width
    spans = ((0, half), (half, half), (2 * half, 2 * half))

    def build(index):
        start, depth = spans[index]

        def one(j, carry):
            cols = pl.ds(pl.multiple_of(j * width, width), width)
            levels = lax.broadcasted_iota(jnp.int32, (depth, width), 0)
            chosen = triples_ref[index : index + 1, cols]
            sel_ref[start : start + depth, cols] = jnp.where(levels == chosen, 1.0, 0.0).astype(jnp.bfloat16)
            if index == 2:
                signs_ref[cols, :] = sketch_ref[cols, :].astype(jnp.float32).astype(jnp.bfloat16)
            return carry

        lax.fori_loop(0, tiles, one, 0)

    own = pltpu.make_async_copy(coeffs_hbm, blocks.at[me], own_sem.at[0])
    own.start()
    triples_copy = pltpu.make_async_copy(triples_hbm, triples_ref, own_sem.at[1])
    triples_copy.start()
    sketch_copy = pltpu.make_async_copy(sketch_hbm, sketch_ref, own_sem.at[2])
    sketch_copy.start()
    peers = peers_of(spot, images)
    greet((("feat", peers_of(me, count)), ("img", peers)))
    own.wait()
    triples_copy.wait()

    def copy(side, hop, chunk, source, target):
        span = blocks.at[source, pl.ds(pl.multiple_of(chunk * step, step), step)]
        return pltpu.make_async_remote_copy(
            src_ref=span,
            dst_ref=span,
            send_sem=send_sem.at[side, hop, chunk],
            recv_sem=recv_sem.at[side, hop, chunk],
            device_id={"feat": target},
            device_id_type=MESH,
        )

    owners = (count // 2 - 1, count // 2)
    piece = step // len(owners)

    def rows_of(chunk, o):
        return pl.ds(pl.multiple_of(chunk * step + o * piece, piece), piece)

    def reduce_copy(o, chunk, sender):
        return pltpu.make_async_remote_copy(
            src_ref=part_ref.at[rows_of(chunk, o)],
            dst_ref=slots.at[sender, chunk],
            send_sem=to_sem.at[o, chunk],
            recv_sem=from_sem.at[sender, chunk],
            device_id={"feat": owners[o]},
            device_id_type=MESH,
        )

    def spread_copy(o, chunk, target):
        span = full_ref.at[rows_of(chunk, o)]
        return pltpu.make_async_remote_copy(
            src_ref=span,
            dst_ref=span,
            send_sem=out_sem.at[target, chunk],
            recv_sem=in_sem.at[o, chunk],
            device_id={"feat": target},
            device_id_type=MESH,
        )

    def send_own(chunk, live):
        @pl.when(live & (me < count - 1))
        def _():
            copy(0, 0, chunk, me, me + 1).start()

        @pl.when(live & (me > 0))
        def _():
            copy(1, 0, chunk, me, me - 1).start()

    for chunk in range(AHEAD):
        send_own(chunk, True)
    gram_ref[...] = jnp.zeros(gram_ref.shape, jnp.float32)
    raw_ref[...] = jnp.zeros(raw_ref.shape, jnp.float32)

    def one_round(turn, carry):
        for hop in range(count):
            chunk = turn - hop
            live = (chunk >= 0) & (chunk < CHUNKS)
            if hop > 0:

                @pl.when(live & (me >= hop))
                def _():
                    copy(0, hop - 1, chunk, me - hop, me - 1).wait_recv()

                @pl.when(live & (me + hop < count))
                def _():
                    copy(1, hop - 1, chunk, me + hop, me + 1).wait_recv()

            if 0 < hop < count - 1:

                @pl.when(live & (me >= hop) & (me < count - 1))
                def _():
                    copy(0, hop, chunk, me - hop, me + 1).start()

                @pl.when(live & (me + hop < count) & (me > 0))
                def _():
                    copy(1, hop, chunk, me + hop, me - 1).start()

        send_own(turn + AHEAD, (turn + AHEAD) < CHUNKS)
        for index in range(3):

            @pl.when(turn == min(index, count - 2))
            def _():
                if index == 2:
                    sketch_copy.wait()
                build(index)

        base = turn - (count - 1)
        for o, owner in enumerate(owners):

            @pl.when((base >= 1) & (base <= CHUNKS) & (me != owner))
            def _():
                reduce_copy(o, base - 1, me).start()

            @pl.when((base >= 2) & (me == owner))
            def _():
                for target in range(count):
                    if target != owner:
                        spread_copy(o, base - 2, target).start()

        @pl.when((base >= 0) & (base < CHUNKS))
        def _():
            here = pl.ds(pl.multiple_of(base * step, step), step)
            sum_ref[...] = jnp.zeros(sum_ref.shape, jnp.float32)
            low = jnp.concatenate([blocks[s, here, :] for s in range(count // 2)], axis=1)
            high = jnp.concatenate([blocks[s, here, :] for s in range(count // 2, count)], axis=1)
            full = jnp.concatenate([low, high], axis=1)

            def one_tile(j, unused):
                cols = pl.ds(pl.multiple_of(j * width, width), width)
                first = jnp.dot(low, sel_ref[:half, cols], preferred_element_type=jnp.float32)
                second = jnp.dot(low, sel_ref[half : 2 * half, cols], preferred_element_type=jnp.float32)
                third = jnp.dot(full, sel_ref[2 * half :, cols], preferred_element_type=jnp.float32)
                tile = (first * second * third).astype(jnp.bfloat16)
                tile_ref[here, cols] = tile
                sum_ref[...] += jnp.dot(tile, signs_ref[cols, :], preferred_element_type=jnp.float32)
                return unused

            lax.fori_loop(0, tiles, one_tile, 0, unroll=2)
            part_ref[here, :] = sum_ref[...].astype(jnp.bfloat16)

        for o, owner in enumerate(owners):

            @pl.when((base >= 1) & (base <= CHUNKS) & (me == owner))
            def _():
                mine = rows_of(base - 1, o)
                total = part_ref[mine, :].astype(jnp.float32)
                for sender in range(count):
                    if sender != owner:
                        reduce_copy(o, base - 1, sender).wait_recv()
                        total = total + slots[sender, base - 1].astype(jnp.float32)
                full_ref[mine, :] = total.astype(jnp.bfloat16)

        for o, owner in enumerate(owners):

            @pl.when((base >= 2) & (me != owner))
            def _():
                spread_copy(o, base - 2, me).wait_recv()

        @pl.when(base >= 2)
        def _():
            here = pl.ds(pl.multiple_of((base - 2) * step, step), step)
            value = full_ref[here, :]
            turned = value.T
            gram_ref[...] += jnp.dot(turned, value, preferred_element_type=jnp.float32)

            def one_tile(j, unused):
                cols = pl.ds(pl.multiple_of(j * width, width), width)
                raw_ref[:, cols] += jnp.dot(turned, tile_ref[here, cols], preferred_element_type=jnp.float32)
                return unused

            lax.fori_loop(0, tiles, one_tile, 0)

        return carry

    lax.fori_loop(0, CHUNKS + count + 1, one_round, 0)

    side = lax.rem(spot, 2)
    pairs = images // 2
    chips = [lax.rem(spot + 2 * k, images) for k in range(1, pairs)]
    span = feats // images
    rank_part = out_ref.shape[0]

    def columns(owner):
        return pl.ds(pl.multiple_of(owner * span, span), span)

    def remote(source, target, send, recv, device):
        return pltpu.make_async_remote_copy(
            src_ref=source, dst_ref=target, send_sem=send, recv_sem=recv, device_id={"img": device}, device_id_type=MESH
        )

    twin = spot + 1 - 2 * side
    gram_pair = remote(gram_ref, pair_gram, gram_send.at[0], gram_recv.at[0], twin)
    gram_pair.start()
    pair_copies = []
    for m in range(pairs):
        pair_staged[m] = raw_ref[:, columns(2 * m + 1 - side)].astype(jnp.bfloat16)
        pair_copies.append(remote(pair_staged.at[m], pair_raw.at[m], pair_send.at[m], pair_recv.at[m], twin))
        pair_copies[-1].start()
    gram_pair.wait_recv()
    chip_gram[0] = gram_ref[...] + pair_gram[...]
    gram_copies = [
        remote(chip_gram.at[0], chip_gram.at[k + 1], gram_send.at[k + 1], gram_recv.at[k + 1], chip)
        for k, chip in enumerate(chips)
    ]
    for one in gram_copies:
        one.start()
    for one in pair_copies:
        one.wait_recv()
    chip_copies = []
    for k, chip in enumerate(chips):
        both = raw_ref[:, columns(chip)] + pair_raw[lax.div(chip, 2)].astype(jnp.float32)
        chip_staged[k] = both.astype(jnp.bfloat16)
        chip_copies.append(remote(chip_staged.at[k], chip_raw.at[k], chip_send.at[k], chip_recv.at[k], chip))
        chip_copies[-1].start()
    for one in gram_copies:
        one.wait_recv()
    total = jnp.zeros(gram_ref.shape, jnp.float32)
    for chip in range(pairs):
        total = total + chip_gram[lax.rem(lax.div(spot, 2) + pairs - chip, pairs)]
    factor_panels(scale, after, total, left, right, pivots, inverse_ref, min(PANEL, total.shape[0]))
    mine = raw_ref[:, columns(spot)] + pair_raw[lax.div(spot, 2)].astype(jnp.float32)
    for k, one in enumerate(chip_copies):
        one.wait_recv()
        mine = mine + chip_raw[k].astype(jnp.float32)
    solved = jnp.dot(inverse_ref[...], mine, precision=lax.Precision.HIGHEST, preferred_element_type=jnp.float32) * root
    solved_ref[...] = solved.astype(jnp.bfloat16)

    def ranks(owner):
        return pl.ds(pl.multiple_of(owner * rank_part, rank_part), rank_part)

    row_copies = [
        remote(solved_ref.at[ranks(peer)], row_slots.at[k], row_send.at[k], row_recv.at[k], peer)
        for k, peer in enumerate(peers)
    ]
    for one in row_copies:
        one.start()
    value_ref[...] = full_ref[...]
    out_ref[:, columns(spot)] = solved_ref[ranks(spot), :].astype(jnp.float32)

    def drain(chunk, carry):
        for o, owner in enumerate(owners):

            @pl.when(me != owner)
            def _():
                reduce_copy(o, chunk, me).wait_send()

            @pl.when(me == owner)
            def _():
                for target in range(count):
                    if target != owner:
                        spread_copy(o, chunk, target).wait_send()

        for hop in range(count - 1):

            @pl.when((me >= hop) & (me < count - 1))
            def _():
                copy(0, hop, chunk, me - hop, me + 1).wait_send()

            @pl.when((me + hop < count) & (me > 0))
            def _():
                copy(1, hop, chunk, me + hop, me - 1).wait_send()

        return carry

    lax.fori_loop(0, CHUNKS, drain, 0)
    for k, one in enumerate(row_copies):
        one.wait_recv()
        out_ref[:, columns(lax.rem(spot + images - 1 - k, images))] = row_slots[k].astype(jnp.float32)
    for one in [gram_pair] + pair_copies + gram_copies + chip_copies + row_copies:
        one.wait_send()


def factor_and_project(coeffs, triples, sketch, count, images, scale, after, root):
    rows, part = coeffs.shape
    feats, rank = sketch.shape
    hops = max(count - 1, 1)
    step = rows // CHUNKS
    pairs = images // 2
    span = feats // images
    rank_part = rank // images
    square = pltpu.VMEM((rank, rank), jnp.float32)
    dma = pltpu.SemaphoreType.DMA
    return pl.pallas_call(
        functools.partial(whole_kernel, count, images, min(1024, feats), scale, after, root),
        in_specs=[HBM] * 3,
        out_specs=[VMEM] * 3,
        out_shape=[
            jax.ShapeDtypeStruct((rows, rank), jnp.bfloat16),
            jax.ShapeDtypeStruct((rank, rank), jnp.float32),
            jax.ShapeDtypeStruct((rank_part, feats), jnp.float32),
        ],
        scratch_shapes=[
            pltpu.VMEM(triples.shape, jnp.int32),
            pltpu.VMEM((feats, rank), jnp.int32),
            pltpu.VMEM((rows, feats), jnp.bfloat16),
            pltpu.VMEM((count, rows, part), jnp.bfloat16),
            pltpu.VMEM((2 * count * part, feats), jnp.bfloat16),
            pltpu.VMEM((feats, rank), jnp.bfloat16),
            pltpu.VMEM((step, rank), jnp.float32),
            pltpu.VMEM((rows, rank), jnp.bfloat16),
            pltpu.VMEM((count, CHUNKS, step // 2, rank), jnp.bfloat16),
            pltpu.VMEM((rows, rank), jnp.bfloat16),
            square,
            pltpu.VMEM((rank, feats), jnp.float32),
            square,
            pltpu.VMEM((pairs, rank, rank), jnp.float32),
            pltpu.VMEM((pairs, rank, span), jnp.bfloat16),
            pltpu.VMEM((pairs, rank, span), jnp.bfloat16),
            pltpu.VMEM((pairs - 1, rank, span), jnp.bfloat16),
            pltpu.VMEM((pairs - 1, rank, span), jnp.bfloat16),
            pltpu.VMEM((rank, span), jnp.bfloat16),
            pltpu.VMEM((images - 1, rank_part, span), jnp.bfloat16),
            square,
            square,
            square,
            dma((3,)),
            dma((2, hops, CHUNKS)),
            dma((2, hops, CHUNKS)),
            dma((2, CHUNKS)),
            dma((count, CHUNKS)),
            dma((count, CHUNKS)),
            dma((2, CHUNKS)),
        ]
        + [dma((pairs,))] * 4
        + [dma((pairs - 1,))] * 2
        + [dma((images - 1,))] * 2,
        compiler_params=pltpu.CompilerParams(
            collective_id=0, has_side_effects=True, vmem_limit_bytes=44 << 20
        ),
    )(*(pltpu.with_memory_space_constraint(array, pltpu.HBM) for array in (coeffs, triples, sketch)))


def on_device(coeffs, triples, sketch):
    rows_here = coeffs.shape[0]
    feats_here = triples.shape[1]
    img_count = lax.axis_size("img")
    feat_count = lax.axis_size("feat")
    total_rows = rows_here * img_count
    total_feats = feats_here * feat_count
    sketch_scale = (1.5 / total_feats) ** 0.5
    value, inverse, projected = factor_and_project(
        coeffs, triples, sketch, feat_count, img_count,
        sketch_scale * sketch_scale / total_rows, sketch_scale, total_rows**-0.5,
    )
    basis = jnp.dot(value.astype(jnp.float32), inverse.T, precision=lax.Precision.HIGHEST)
    return (basis, projected)


def solution(mesh):
    in_specs = (P("img", "feat"), P(None, "feat"), P("feat", None))
    out_specs = (P("img", None), P("img", "feat"))
    return jax.shard_map(
        on_device, mesh=mesh, in_specs=in_specs, out_specs=out_specs, check_vma=False
    )
```

time: 117 us -> 95.7 us (0.82)
  Pallas kernels: 108 us -> 92.6 us
  local copies, waits for them, and re-layouts: 4.17 us -> 0.7 us
  matrix products: 3.48 us -> 1.57 us
    pallas_call x4 -> x1, Pallas kernels: 108 us -> 92.6 us  [factor_and_project(): pl.pallas_call(functools.partial(whole_kernel, count, images, min(1024, f...]
    unnamed x7 -> x1, local copies, waits for them, and re-layouts: 4.17 us -> 0.7 us
    dot_general x2 -> x1, matrix products: 3.48 us -> 1.57 us  [on_device(): jnp.dot(value.astype(jnp.float32), inverse.T, precision=lax.Precision.HIG...]
where the time goes in v3:
time: 95.7 us; the launch traced here: 95.5 us
  Pallas kernels  92.6 us (97%)
  matrix products  1.57 us (2%)
    pallas_call x1, Pallas kernels, factor_and_project(): pl.pallas_call(functools.partial(whole_kernel, count, images, min(1024, f...  92.6 us

profile of v3, /device:TPU:0, one launch (start us, length us, event | category | flops | bytes accessed | tf_op | source)
XLA Modules:
  0.0 95.5 jit_solution(6127744468171158604)
XLA Ops:
  0.6 92.6 %shard_map.50 = (bf16[2048,128]{1,0:T(8,128)(2,1)S(1)}, f32[128,128]{1,0:T(8,128)S(1)}, f32[16,4096]{1,0:T(8,128)S(1)}) custom-call(bf16[2048,128]{1,0:T(8,128)(2,1)} %coeffs_hbm.1, s32[3,4096]{1,0:T(4,128)} %triples_hbm.1, s32[4096,128]{1,0:T(8,128)} %sketch_hbm.1), custom_call_target="tpu_custom_call" | custom-call | tf_op jit(solution)/shard_map/pallas_call | solution.py:380
  93.3 1.6 %fusion = f32[2048,128]{1,0:T(8,128)} fusion(bf16[2048,128]{1,0:T(8,128)(2,1)S(1)} %get-tuple-element.5, f32[128,128]{1,0:T(8,128)S(1)} %get-tuple-element.6), kind=kOutput, calls=%fused_computation | convolution fusion | flops 402653184 | bytes 1638400 | tf_op jit(solution)/shard_map/dot_general | solution.py:442
  94.8 0.7 copy.6

commit v4 on v3

--- a/solution.py
+++ b/solution.py
@@ -208,8 +208,15 @@
             def _():
                 reduce_copy(o, base - 1, me).start()
 
-            @pl.when((base >= 2) & (me == owner))
-            def _():
+            @pl.when((base >= 2) & (base <= CHUNKS + 1) & (me == owner))
+            def _():
+                mine = rows_of(base - 2, o)
+                total = part_ref[mine, :].astype(jnp.float32)
+                for sender in range(count):
+                    if sender != owner:
+                        reduce_copy(o, base - 2, sender).wait_recv()
+                        total = total + slots[sender, base - 2].astype(jnp.float32)
+                full_ref[mine, :] = total.astype(jnp.bfloat16)
                 for target in range(count):
                     if target != owner:
                         spread_copy(o, base - 2, target).start()
@@ -237,25 +244,13 @@
 
         for o, owner in enumerate(owners):
 
-            @pl.when((base >= 1) & (base <= CHUNKS) & (me == owner))
-            def _():
-                mine = rows_of(base - 1, o)
-                total = part_ref[mine, :].astype(jnp.float32)
-                for sender in range(count):
-                    if sender != owner:
-                        reduce_copy(o, base - 1, sender).wait_recv()
-                        total = total + slots[sender, base - 1].astype(jnp.float32)
-                full_ref[mine, :] = total.astype(jnp.bfloat16)
-
-        for o, owner in enumerate(owners):
-
-            @pl.when((base >= 2) & (me != owner))
-            def _():
-                spread_copy(o, base - 2, me).wait_recv()
-
-        @pl.when(base >= 2)
+            @pl.when((base >= 3) & (me != owner))
+            def _():
+                spread_copy(o, base - 3, me).wait_recv()
+
+        @pl.when(base >= 3)
         def _():
-            here = pl.ds(pl.multiple_of((base - 2) * step, step), step)
+            here = pl.ds(pl.multiple_of((base - 3) * step, step), step)
             value = full_ref[here, :]
             turned = value.T
             gram_ref[...] += jnp.dot(turned, value, preferred_element_type=jnp.float32)
@@ -269,7 +264,7 @@
 
         return carry
 
-    lax.fori_loop(0, CHUNKS + count + 1, one_round, 0)
+    lax.fori_loop(0, CHUNKS + count + 2, one_round, 0)
 
     side = lax.rem(spot, 2)
     pairs = images // 2

time: 95.7 us -> 83.3 us (0.87)
  Pallas kernels: 92.6 us -> 80.3 us
    pallas_call x1, Pallas kernels: 92.6 us -> 80.3 us  [factor_and_project(): pl.pallas_call(functools.partial(whole_kernel, count, images, min(1024, f...]
where the time goes in v4:
time: 83.3 us; the launch traced here: 83.2 us
  Pallas kernels  80.3 us (96%)
  matrix products  1.57 us (2%)
    pallas_call x1, Pallas kernels, factor_and_project(): pl.pallas_call(functools.partial(whole_kernel, count, images, min(1024, f...  80.3 us

profile of v4, /device:TPU:0, one launch (start us, length us, event | category | flops | bytes accessed | tf_op | source)
XLA Modules:
  0.0 83.2 jit_solution(6202830912856496858)
XLA Ops:
  0.6 80.3 %shard_map.50 = (bf16[2048,128]{1,0:T(8,128)(2,1)S(1)}, f32[128,128]{1,0:T(8,128)S(1)}, f32[16,4096]{1,0:T(8,128)S(1)}) custom-call(bf16[2048,128]{1,0:T(8,128)(2,1)} %coeffs_hbm.1, s32[3,4096]{1,0:T(4,128)} %triples_hbm.1, s32[4096,128]{1,0:T(8,128)} %sketch_hbm.1), custom_call_target="tpu_custom_call" | custom-call | tf_op jit(solution)/shard_map/pallas_call | solution.py:375
  80.9 1.6 %fusion = f32[2048,128]{1,0:T(8,128)} fusion(bf16[2048,128]{1,0:T(8,128)(2,1)S(1)} %get-tuple-element.5, f32[128,128]{1,0:T(8,128)S(1)} %get-tuple-element.6), kind=kOutput, calls=%fused_computation | convolution fusion | flops 402653184 | bytes 1638400 | tf_op jit(solution)/shard_map/dot_general | solution.py:437
  82.5 0.7 copy.6

commit v5 on v4

--- a/solution.py
+++ b/solution.py
@@ -8,7 +8,9 @@
 from jax.sharding import PartitionSpec as P
 
 CHUNKS = 8
-AHEAD = 2
+AHEAD = (4, 1)
+SUMMED = 5
+SPREAD = 7
 SUB = 8
 PANEL = 32
 MESH = pl.DeviceIdType.MESH
@@ -163,8 +165,9 @@
         def _():
             copy(1, 0, chunk, me, me - 1).start()
 
-    for chunk in range(AHEAD):
-        send_own(chunk, True)
+    ahead = AHEAD[0] + (AHEAD[1] - AHEAD[0]) * lax.rem(spot, 2)
+    for chunk in range(max(AHEAD)):
+        send_own(chunk, chunk < ahead)
     gram_ref[...] = jnp.zeros(gram_ref.shape, jnp.float32)
     raw_ref[...] = jnp.zeros(raw_ref.shape, jnp.float32)
 
@@ -192,7 +195,7 @@
                 def _():
                     copy(1, hop, chunk, me + hop, me - 1).start()
 
-        send_own(turn + AHEAD, (turn + AHEAD) < CHUNKS)
+        send_own(turn + ahead, (turn + ahead) < CHUNKS)
         for index in range(3):
 
             @pl.when(turn == min(index, count - 2))
@@ -208,18 +211,18 @@
             def _():
                 reduce_copy(o, base - 1, me).start()
 
-            @pl.when((base >= 2) & (base <= CHUNKS + 1) & (me == owner))
-            def _():
-                mine = rows_of(base - 2, o)
+            @pl.when((base >= SUMMED) & (base <= CHUNKS + SUMMED - 1) & (me == owner))
+            def _():
+                mine = rows_of(base - SUMMED, o)
                 total = part_ref[mine, :].astype(jnp.float32)
                 for sender in range(count):
                     if sender != owner:
-                        reduce_copy(o, base - 2, sender).wait_recv()
-                        total = total + slots[sender, base - 2].astype(jnp.float32)
+                        reduce_copy(o, base - SUMMED, sender).wait_recv()
+                        total = total + slots[sender, base - SUMMED].astype(jnp.float32)
                 full_ref[mine, :] = total.astype(jnp.bfloat16)
                 for target in range(count):
                     if target != owner:
-                        spread_copy(o, base - 2, target).start()
+                        spread_copy(o, base - SUMMED, target).start()
 
         @pl.when((base >= 0) & (base < CHUNKS))
         def _():
@@ -244,13 +247,13 @@
 
         for o, owner in enumerate(owners):
 
-            @pl.when((base >= 3) & (me != owner))
-            def _():
-                spread_copy(o, base - 3, me).wait_recv()
-
-        @pl.when(base >= 3)
-        def _():
-            here = pl.ds(pl.multiple_of((base - 3) * step, step), step)
+            @pl.when((base >= SPREAD) & (me != owner))
+            def _():
+                spread_copy(o, base - SPREAD, me).wait_recv()
+
+        @pl.when(base >= SPREAD)
+        def _():
+            here = pl.ds(pl.multiple_of((base - SPREAD) * step, step), step)
             value = full_ref[here, :]
             turned = value.T
             gram_ref[...] += jnp.dot(turned, value, preferred_element_type=jnp.float32)
@@ -264,7 +267,13 @@
 
         return carry
 
-    lax.fori_loop(0, CHUNKS + count + 2, one_round, 0)
+    lax.fori_loop(0, CHUNKS + count - 2 + SPREAD, one_round, 0)
+    for o, owner in enumerate(owners):
+
+        @pl.when(me != owner)
+        def _():
+            spread_copy(o, CHUNKS - 1, me).wait_recv()
+
 
     side = lax.rem(spot, 2)
     pairs = images // 2
@@ -281,12 +290,24 @@
         )
 
     twin = spot + 1 - 2 * side
+    mate = lax.div(spot, 2)
+    order = [lax.rem(mate + k, pairs) for k in range(1, pairs + 1)]
+    last = pl.ds((CHUNKS - 1) * step, step)
+    value = full_ref[last, :]
+    turned = value.T
+
+    def raw_of(owner):
+        return raw_ref[:, columns(owner)] + jnp.dot(
+            turned, tile_ref[last, columns(owner)], preferred_element_type=jnp.float32
+        )
+
+    gram_ref[...] += jnp.dot(turned, value, preferred_element_type=jnp.float32)
     gram_pair = remote(gram_ref, pair_gram, gram_send.at[0], gram_recv.at[0], twin)
     gram_pair.start()
     pair_copies = []
-    for m in range(pairs):
-        pair_staged[m] = raw_ref[:, columns(2 * m + 1 - side)].astype(jnp.bfloat16)
-        pair_copies.append(remote(pair_staged.at[m], pair_raw.at[m], pair_send.at[m], pair_recv.at[m], twin))
+    for k, m in enumerate(order):
+        pair_staged[k] = raw_of(2 * m + 1 - side).astype(jnp.bfloat16)
+        pair_copies.append(remote(pair_staged.at[k], pair_raw.at[k], pair_send.at[k], pair_recv.at[k], twin))
         pair_copies[-1].start()
     gram_pair.wait_recv()
     chip_gram[0] = gram_ref[...] + pair_gram[...]
@@ -296,21 +317,22 @@
     ]
     for one in gram_copies:
         one.start()
-    for one in pair_copies:
-        one.wait_recv()
     chip_copies = []
     for k, chip in enumerate(chips):
-        both = raw_ref[:, columns(chip)] + pair_raw[lax.div(chip, 2)].astype(jnp.float32)
-        chip_staged[k] = both.astype(jnp.bfloat16)
+        both = raw_of(chip)
+        pair_copies[k].wait_recv()
+        chip_staged[k] = (both + pair_raw[k].astype(jnp.float32)).astype(jnp.bfloat16)
         chip_copies.append(remote(chip_staged.at[k], chip_raw.at[k], chip_send.at[k], chip_recv.at[k], chip))
         chip_copies[-1].start()
+    mine = raw_of(spot)
+    pair_copies[-1].wait_recv()
+    mine = mine + pair_raw[pairs - 1].astype(jnp.float32)
     for one in gram_copies:
         one.wait_recv()
     total = jnp.zeros(gram_ref.shape, jnp.float32)
     for chip in range(pairs):
         total = total + chip_gram[lax.rem(lax.div(spot, 2) + pairs - chip, pairs)]
     factor_panels(scale, after, total, left, right, pivots, inverse_ref, min(PANEL, total.shape[0]))
-    mine = raw_ref[:, columns(spot)] + pair_raw[lax.div(spot, 2)].astype(jnp.float32)
     for k, one in enumerate(chip_copies):
         one.wait_recv()
         mine = mine + chip_raw[k].astype(jnp.float32)

time: 83.3 us -> 78.2 us (0.939)
  Pallas kernels: 80.3 us -> 75.1 us
    pallas_call x1, Pallas kernels: 80.3 us -> 75.1 us  [factor_and_project(): pl.pallas_call(functools.partial(whole_kernel, count, images, min(1024, f...]
where the time goes in v5:
time: 78.2 us; the launch traced here: 78 us
  Pallas kernels  75.1 us (96%)
  matrix products  1.57 us (2%)
    pallas_call x1, Pallas kernels, factor_and_project(): pl.pallas_call(functools.partial(whole_kernel, count, images, min(1024, f...  75.1 us
    dot_general x1, matrix products, on_device(): jnp.dot(value.astype(jnp.float32), inverse.T, precision=lax.Precision.HIG...  1.57 us

profile of v5, /device:TPU:0, one launch (start us, length us, event | category | flops | bytes accessed | tf_op | source)
XLA Modules:
  0.0 78.0 jit_solution(10466445521593140105)
XLA Ops:
  0.6 75.1 %shard_map.50 = (bf16[2048,128]{1,0:T(8,128)(2,1)S(1)}, f32[128,128]{1,0:T(8,128)S(1)}, f32[16,4096]{1,0:T(8,128)S(1)}) custom-call(bf16[2048,128]{1,0:T(8,128)(2,1)} %coeffs_hbm.1, s32[3,4096]{1,0:T(4,128)} %triples_hbm.1, s32[4096,128]{1,0:T(8,128)} %sketch_hbm.1), custom_call_target="tpu_custom_call" | custom-call | tf_op jit(solution)/shard_map/pallas_call | solution.py:397
  75.8 1.6 %fusion = f32[2048,128]{1,0:T(8,128)} fusion(bf16[2048,128]{1,0:T(8,128)(2,1)S(1)} %get-tuple-element.5, f32[128,128]{1,0:T(8,128)S(1)} %get-tuple-element.6), kind=kOutput, calls=%fused_computation | convolution fusion | flops 402653184 | bytes 1638400 | tf_op jit(solution)/shard_map/dot_general | solution.py:459
  77.3 0.7 copy.6

commit v6 on v5

--- a/solution.py
+++ b/solution.py
@@ -13,6 +13,7 @@
 SPREAD = 7
 SUB = 8
 PANEL = 32
+PIECES = 4
 MESH = pl.DeviceIdType.MESH
 VMEM = pl.BlockSpec(memory_space=pltpu.VMEM)
 HBM = pl.BlockSpec(memory_space=pltpu.HBM)
@@ -78,9 +79,9 @@
 
 
 def whole_kernel(
-    count, images, width, scale, after, root, coeffs_hbm, triples_hbm, sketch_hbm, value_ref, inverse_ref, out_ref,
+    count, images, width, scale, after, root, coeffs_hbm, triples_hbm, sketch_hbm, basis_ref, out_ref,
     triples_ref, sketch_ref, tile_ref, blocks, sel_ref, signs_ref, sum_ref, part_ref, slots, full_ref, gram_ref,
-    raw_ref, pair_gram, chip_gram, pair_staged, pair_raw, chip_staged, chip_raw, solved_ref, row_slots, left, right,
+    inverse_ref, raw_ref, pair_gram, chip_gram, pair_staged, pair_raw, chip_staged, chip_raw, solved_ref, row_slots, left, right,
     pivots, own_sem, send_sem, recv_sem, to_sem, from_sem, out_sem, in_sem, gram_send, gram_recv, pair_send, pair_recv,
     chip_send, chip_recv, row_send, row_recv
 ):
@@ -348,7 +349,22 @@
     ]
     for one in row_copies:
         one.start()
-    value_ref[...] = full_ref[...]
+    high = inverse_ref[...].astype(jnp.bfloat16)
+    rest = inverse_ref[...] - high.astype(jnp.float32)
+    middle = rest.astype(jnp.bfloat16)
+    low = (rest - middle.astype(jnp.float32)).astype(jnp.bfloat16)
+    turn_back = (((1,), (1,)), ((), ()))
+
+    def one_block(j, carry):
+        here = pl.ds(pl.multiple_of(j * step, step), step)
+        block = full_ref[here, :]
+        made = [
+            lax.dot_general(block, piece, turn_back, preferred_element_type=jnp.float32) for piece in (low, middle, high)
+        ]
+        basis_ref[here, :] = made[0] + made[1] + made[2]
+        return carry
+
+    lax.fori_loop(0, CHUNKS, one_block, 0)
     out_ref[:, columns(spot)] = solved_ref[ranks(spot), :].astype(jnp.float32)
 
     def drain(chunk, carry):
@@ -397,10 +413,9 @@
     return pl.pallas_call(
         functools.partial(whole_kernel, count, images, min(1024, feats), scale, after, root),
         in_specs=[HBM] * 3,
-        out_specs=[VMEM] * 3,
+        out_specs=[VMEM] * 2,
         out_shape=[
-            jax.ShapeDtypeStruct((rows, rank), jnp.bfloat16),
-            jax.ShapeDtypeStruct((rank, rank), jnp.float32),
+            jax.ShapeDtypeStruct((rows, rank), jnp.float32),
             jax.ShapeDtypeStruct((rank_part, feats), jnp.float32),
         ],
         scratch_shapes=[
@@ -414,6 +429,7 @@
             pltpu.VMEM((rows, rank), jnp.bfloat16),
             pltpu.VMEM((count, CHUNKS, step // 2, rank), jnp.bfloat16),
             pltpu.VMEM((rows, rank), jnp.bfloat16),
+            square,
             square,
             pltpu.VMEM((rank, feats), jnp.float32),
             square,
@@ -444,6 +460,29 @@
     )(*(pltpu.with_memory_space_constraint(array, pltpu.HBM) for array in (coeffs, triples, sketch)))
 
 
+def hand_out_kernel(basis_ref, part_ref, basis_hbm, part_hbm, sems):
+    step = basis_ref.shape[0] // PIECES
+    copies = [pltpu.make_async_copy(part_ref, part_hbm, sems.at[PIECES])]
+    for k in range(PIECES):
+        here = pl.ds(k * step, step)
+        copies.append(pltpu.make_async_copy(basis_ref.at[here], basis_hbm.at[here], sems.at[k]))
+    for one in copies:
+        one.start()
+    for one in copies:
+        one.wait()
+
+
+def hand_out(basis, part):
+    return pl.pallas_call(
+        hand_out_kernel,
+        in_specs=[VMEM] * 2,
+        out_specs=[HBM] * 2,
+        out_shape=[jax.ShapeDtypeStruct(basis.shape, basis.dtype), jax.ShapeDtypeStruct(part.shape, part.dtype)],
+        scratch_shapes=[pltpu.SemaphoreType.DMA((PIECES + 1,))],
+        compiler_params=pltpu.CompilerParams(vmem_limit_bytes=4 << 20),
+    )(basis, part)
+
+
 def on_device(coeffs, triples, sketch):
     rows_here = coeffs.shape[0]
     feats_here = triples.shape[1]
@@ -452,12 +491,10 @@
     total_rows = rows_here * img_count
     total_feats = feats_here * feat_count
     sketch_scale = (1.5 / total_feats) ** 0.5
-    value, inverse, projected = factor_and_project(
+    return hand_out(*factor_and_project(
         coeffs, triples, sketch, feat_count, img_count,
         sketch_scale * sketch_scale / total_rows, sketch_scale, total_rows**-0.5,
-    )
-    basis = jnp.dot(value.astype(jnp.float32), inverse.T, precision=lax.Precision.HIGHEST)
-    return (basis, projected)
+    ))
 
 
 def solution(mesh):

time: 78.2 us -> 77.3 us (0.988)
  matrix products: 1.57 us -> 0 us
  Pallas kernels: 75.1 us -> 76.5 us
    dot_general x1 -> x0, matrix products: 1.57 us -> none  [on_device(): jnp.dot(value.astype(jnp.float32), inverse.T, precision=lax.Precision.HIG...]
    pallas_call x0 -> x1, Pallas kernels: none -> 1.09 us  [hand_out(): pl.pallas_call(hand_out_kernel, in_specs=[VMEM] * 2, out_specs=[HBM] * 2,...]
where the time goes in v6:
time: 77.3 us; the launch traced here: 77.1 us
  Pallas kernels  76.5 us (99%)
    pallas_call x1, Pallas kernels, factor_and_project(): pl.pallas_call(functools.partial(whole_kernel, count, images, min(1024, f...  75.4 us

profile of v6, /device:TPU:0, one launch (start us, length us, event | category | flops | bytes accessed | tf_op | source)
XLA Modules:
  0.0 77.1 jit_solution(14478737315106203093)
XLA Ops:
  0.6 75.4 %shard_map.50 = (f32[2048,128]{1,0:T(8,128)S(1)}, f32[16,4096]{1,0:T(8,128)S(1)}) custom-call(bf16[2048,128]{1,0:T(8,128)(2,1)} %coeffs_hbm.1, s32[3,4096]{1,0:T(4,128)} %triples_hbm.1, s32[4096,128]{1,0:T(8,128)} %sketch_hbm.1), custom_call_target="tpu_custom_call" | custom-call | tf_op jit(solution)/shard_map/pallas_call | solution.py:413
  76.0 1.1 %shard_map.51 = (f32[2048,128]{1,0:T(8,128)}, f32[16,4096]{1,0:T(8,128)}) custom-call(f32[2048,128]{1,0:T(8,128)S(1)} %get-tuple-element.4.basis_ref, f32[16,4096]{1,0:T(8,128)S(1)} %get-tuple-element.5.part_ref), custom_call_target="tpu_custom_call" | custom-call | tf_op jit(solution)/shard_map/pallas_call | solution.py:476

commit v7 on v6

--- a/solution.py
+++ b/solution.py
@@ -9,8 +9,8 @@
 
 CHUNKS = 8
 AHEAD = (4, 1)
-SUMMED = 5
-SPREAD = 7
+SUMMED = 4
+EARLY = 3
 SUB = 8
 PANEL = 32
 PIECES = 4
@@ -169,8 +169,30 @@
     ahead = AHEAD[0] + (AHEAD[1] - AHEAD[0]) * lax.rem(spot, 2)
     for chunk in range(max(AHEAD)):
         send_own(chunk, chunk < ahead)
-    gram_ref[...] = jnp.zeros(gram_ref.shape, jnp.float32)
-    raw_ref[...] = jnp.zeros(raw_ref.shape, jnp.float32)
+
+    def arrive(chunk):
+        for o, owner in enumerate(owners):
+
+            @pl.when(me != owner)
+            def _():
+                spread_copy(o, chunk, me).wait_recv()
+
+    def add_up(start, stop):
+        for chunk in range(start, stop):
+            arrive(chunk)
+        here = pl.ds(start * step, (stop - start) * step)
+        value = full_ref[here, :]
+        turned = value.T
+        gram = jnp.dot(turned, value, preferred_element_type=jnp.float32)
+        gram_ref[...] = gram if start == 0 else gram_ref[...] + gram
+
+        def one_tile(j, unused):
+            cols = pl.ds(pl.multiple_of(j * width, width), width)
+            raw = jnp.dot(turned, tile_ref[here, cols], preferred_element_type=jnp.float32)
+            raw_ref[:, cols] = raw if start == 0 else raw_ref[:, cols] + raw
+            return unused
+
+        lax.fori_loop(0, tiles, one_tile, 0)
 
     def one_round(turn, carry):
         for hop in range(count):
@@ -246,36 +268,15 @@
             lax.fori_loop(0, tiles, one_tile, 0, unroll=2)
             part_ref[here, :] = sum_ref[...].astype(jnp.bfloat16)
 
-        for o, owner in enumerate(owners):
-
-            @pl.when((base >= SPREAD) & (me != owner))
-            def _():
-                spread_copy(o, base - SPREAD, me).wait_recv()
-
-        @pl.when(base >= SPREAD)
+        @pl.when(base == CHUNKS)
         def _():
-            here = pl.ds(pl.multiple_of((base - SPREAD) * step, step), step)
-            value = full_ref[here, :]
-            turned = value.T
-            gram_ref[...] += jnp.dot(turned, value, preferred_element_type=jnp.float32)
-
-            def one_tile(j, unused):
-                cols = pl.ds(pl.multiple_of(j * width, width), width)
-                raw_ref[:, cols] += jnp.dot(turned, tile_ref[here, cols], preferred_element_type=jnp.float32)
-                return unused
-
-            lax.fori_loop(0, tiles, one_tile, 0)
+            add_up(0, EARLY)
 
         return carry
 
-    lax.fori_loop(0, CHUNKS + count - 2 + SPREAD, one_round, 0)
-    for o, owner in enumerate(owners):
-
-        @pl.when(me != owner)
-        def _():
-            spread_copy(o, CHUNKS - 1, me).wait_recv()
-
-
+    lax.fori_loop(0, CHUNKS + count - 1 + SUMMED, one_round, 0)
+    add_up(EARLY, CHUNKS - 1)
+    arrive(CHUNKS - 1)
     side = lax.rem(spot, 2)
     pairs = images // 2
     chips = [lax.rem(spot + 2 * k, images) for k in range(1, pairs)]

time: 77.3 us -> 75.6 us (0.978)
  Pallas kernels: 76.5 us -> 74.9 us
    pallas_call x1, Pallas kernels: 75.4 us -> 73.8 us  [factor_and_project(): pl.pallas_call(functools.partial(whole_kernel, count, images, min(1024, f...]
where the time goes in v7:
time: 75.6 us; the launch traced here: 75.5 us
  Pallas kernels  74.9 us (99%)
    pallas_call x1, Pallas kernels, factor_and_project(): pl.pallas_call(functools.partial(whole_kernel, count, images, min(1024, f...  73.8 us

profile of v7, /device:TPU:0, one launch (start us, length us, event | category | flops | bytes accessed | tf_op | source)
XLA Modules:
  0.0 75.5 jit_solution(12784418392870165028)
XLA Ops:
  0.6 73.8 %shard_map.50 = (f32[2048,128]{1,0:T(8,128)S(1)}, f32[16,4096]{1,0:T(8,128)S(1)}) custom-call(bf16[2048,128]{1,0:T(8,128)(2,1)} %coeffs_hbm.1, s32[3,4096]{1,0:T(4,128)} %triples_hbm.1, s32[4096,128]{1,0:T(8,128)} %sketch_hbm.1), custom_call_target="tpu_custom_call" | custom-call | tf_op jit(solution)/shard_map/pallas_call | solution.py:414
  74.4 1.1 %shard_map.51 = (f32[2048,128]{1,0:T(8,128)}, f32[16,4096]{1,0:T(8,128)}) custom-call(f32[2048,128]{1,0:T(8,128)S(1)} %get-tuple-element.4.basis_ref, f32[16,4096]{1,0:T(8,128)S(1)} %get-tuple-element.5.part_ref), custom_call_target="tpu_custom_call" | custom-call | tf_op jit(solution)/shard_map/pallas_call | solution.py:477

commit v8 on v7

--- a/solution.py
+++ b/solution.py
@@ -8,7 +8,7 @@
 from jax.sharding import PartitionSpec as P
 
 CHUNKS = 8
-AHEAD = (4, 1)
+AHEAD = (3, 1)
 SUMMED = 4
 EARLY = 3
 SUB = 8
@@ -265,7 +265,7 @@
                 sum_ref[...] += jnp.dot(tile, signs_ref[cols, :], preferred_element_type=jnp.float32)
                 return unused
 
-            lax.fori_loop(0, tiles, one_tile, 0, unroll=2)
+            lax.fori_loop(0, tiles, one_tile, 0, unroll=4)
             part_ref[here, :] = sum_ref[...].astype(jnp.bfloat16)
 
         @pl.when(base == CHUNKS)

time: 75.6 us -> 74.8 us (0.989)
  Pallas kernels: 74.9 us -> 74.1 us
    pallas_call x1, Pallas kernels: 73.8 us -> 73 us  [factor_and_project(): pl.pallas_call(functools.partial(whole_kernel, count, images, min(1024, f...]
where the time goes in v8:
time: 74.8 us; the launch traced here: 74.7 us
  Pallas kernels  74.1 us (99%)
    pallas_call x1, Pallas kernels, factor_and_project(): pl.pallas_call(functools.partial(whole_kernel, count, images, min(1024, f...  73 us

profile of v8, /device:TPU:0, one launch (start us, length us, event | category | flops | bytes accessed | tf_op | source)
XLA Modules:
  0.0 74.7 jit_solution(12388473422602499708)
XLA Ops:
  0.6 73.0 %shard_map.50 = (f32[2048,128]{1,0:T(8,128)S(1)}, f32[16,4096]{1,0:T(8,128)S(1)}) custom-call(bf16[2048,128]{1,0:T(8,128)(2,1)} %coeffs_hbm.1, s32[3,4096]{1,0:T(4,128)} %triples_hbm.1, s32[4096,128]{1,0:T(8,128)} %sketch_hbm.1), custom_call_target="tpu_custom_call" | custom-call | tf_op jit(solution)/shard_map/pallas_call | solution.py:414
  73.6 1.1 %shard_map.51 = (f32[2048,128]{1,0:T(8,128)}, f32[16,4096]{1,0:T(8,128)}) custom-call(f32[2048,128]{1,0:T(8,128)S(1)} %get-tuple-element.4.basis_ref, f32[16,4096]{1,0:T(8,128)S(1)} %get-tuple-element.5.part_ref), custom_call_target="tpu_custom_call" | custom-call | tf_op jit(solution)/shard_map/pallas_call | solution.py:477

commit v9 on v8

--- a/solution.py
+++ b/solution.py
@@ -9,8 +9,8 @@
 
 CHUNKS = 8
 AHEAD = (3, 1)
-SUMMED = 4
-EARLY = 3
+SUMMED = 5
+EARLY = 2
 SUB = 8
 PANEL = 32
 PIECES = 4

time: 74.8 us -> 74.1 us (level)
  no operation moved by 1% of the time
where the time goes in v9:
time: 74.1 us; the launch traced here: 74 us
  Pallas kernels  73.4 us (99%)
    pallas_call x1, Pallas kernels, factor_and_project(): pl.pallas_call(functools.partial(whole_kernel, count, images, min(1024, f...  72.3 us

profile of v9, /device:TPU:0, one launch (start us, length us, event | category | flops | bytes accessed | tf_op | source)
XLA Modules:
  0.0 74.0 jit_solution(8080198801685448073)
XLA Ops:
  0.6 72.3 %shard_map.50 = (f32[2048,128]{1,0:T(8,128)S(1)}, f32[16,4096]{1,0:T(8,128)S(1)}) custom-call(bf16[2048,128]{1,0:T(8,128)(2,1)} %coeffs_hbm.1, s32[3,4096]{1,0:T(4,128)} %triples_hbm.1, s32[4096,128]{1,0:T(8,128)} %sketch_hbm.1), custom_call_target="tpu_custom_call" | custom-call | tf_op jit(solution)/shard_map/pallas_call | solution.py:414
  72.9 1.1 %shard_map.51 = (f32[2048,128]{1,0:T(8,128)}, f32[16,4096]{1,0:T(8,128)}) custom-call(f32[2048,128]{1,0:T(8,128)S(1)} %get-tuple-element.4.basis_ref, f32[16,4096]{1,0:T(8,128)S(1)} %get-tuple-element.5.part_ref), custom_call_target="tpu_custom_call" | custom-call | tf_op jit(solution)/shard_map/pallas_call | solution.py:477
